TPU v7x, 512 devices: a whole 4x4x16 slice. The times are simulated.
512 devices in a mesh: row: 16 (over x, y), col: 32 (over z, core).
Axes of the slice: x: 4, y: 4, z: 16, core: 2. Of those that a mesh axis runs over, the one named last changes fastest.
Arguments:
- rhs: float32 [6144, 12288], P('row', 'col'), may hold values from -6 to 6
- a_pair: float32 [6144, 24576], P('row', 'col'), may hold values from -0.15625 to 0.15625
- b_pair: float32 [12288, 12288], P('row', 'col'), may hold values from -0.15625 to 0.15625
- u_cay: float32 [6144, 384], P('row'), may hold values from -1 to 1, as said below
- v_cay: float32 [384, 12288], P(None, 'col'), may hold values from -1 to 1, as said below
Outputs:
- solved: float32 [6144, 12288], P('row', 'col')
Inputs may be any that keep to these rules, and one draw needn't show every extreme that they name: `u_cay`: each 384 x 384 block of rows has spectral radius below 1. `v_cay`: each 384 x 384 block of columns has spectral radius below 1.
All inputs are finite; a program needn't handle non-finite values.
Results may differ from a plain program's by a relative error of at most 0.0001.
Values sent between devices are 32-bit elements; how exact they have to be, the bound alone decides.
No kernel may reach another device: no remote copies, remote signals or barrier semaphores. Data moves between devices by JAX's collectives and lax.ppermute only.
A program may use at most 64 MiB of HBM per device.

v0:
```python
import jax
import jax.numpy as jnp
from jax import lax
from jax.sharding import PartitionSpec as P

ITERS = 3
precise = lax.Precision.HIGHEST


def from_root(value, axis, source):
    kept = jnp.where(lax.axis_index(axis) == source, value, 0).astype(value.dtype)
    return lax.psum(kept, axis)


def product(left_side, right_side):
    return jnp.dot(left_side, right_side, precision=precise, preferred_element_type=jnp.float32)


def powers(matrix):
    result = [matrix]
    for step_index in range(ITERS - 1):
        result.append(product(result[-1], result[-1]))
    return result


def doubling(u_powers, v_powers, right_side):
    scaled = right_side + product(u_powers[0], right_side)
    iterate = 0.5 * (scaled + product(scaled, v_powers[0]))
    for u_power, v_power in zip(u_powers, v_powers):
        iterate = iterate + product(u_power, product(iterate, v_power))
    return iterate


def body(rhs, a_pair, b_pair, u_cay, v_cay):
    row_index = lax.axis_index("row")
    col_index = lax.axis_index("col")
    row_count = lax.axis_size("row")
    front_sum = lax.axis_size("row") - 1
    block_sum = row_index + col_index
    block_order = rhs.shape[0]
    a_first = a_pair[:, :block_order]
    a_second = a_pair[:, block_order:]
    b_first = b_pair[:block_order]
    b_second = b_pair[block_order:]
    on_first = block_sum == front_sum
    on_second = block_sum == front_sum + 1
    on_trail = block_sum >= front_sum + 2
    empty = jnp.zeros_like(rhs)
    first_x = lax.cond(on_first, lambda: doubling(powers(u_cay), powers(v_cay), rhs), lambda: empty)
    first_down = jax.tree.map(
        lambda part: from_root(part, "row", jnp.clip(front_sum - col_index, 0, row_count - 1)),
        first_x,
    )
    first_across = jax.tree.map(lambda part: from_root(part, "col", front_sum - row_index), first_x)
    from_above = first_down
    from_above = jnp.where(row_index >= 1, from_above, empty)

    def solve_second():
        u_powers, v_powers = (powers(u_cay), powers(v_cay))
        right_side = rhs - (product(a_first, from_above) + product(first_across, b_first))
        return doubling(u_powers, v_powers, right_side)

    second_x = lax.cond(on_second, solve_second, lambda: empty)
    down_root = jnp.clip(front_sum + 1 - col_index, 0, row_count - 1)
    across_root = front_sum + 1 - row_index
    down_pair = (first_down, jax.tree.map(lambda part: from_root(part, "row", down_root), second_x))
    across_pair = (
        first_across,
        jax.tree.map(lambda part: from_root(part, "col", across_root), second_x),
    )
    first_valid = (front_sum - col_index >= 0) & (front_sum - col_index < row_count)
    second_valid = (front_sum + 1 - col_index >= 0) & (front_sum + 1 - col_index < row_count)

    def update_trail():
        upper_first = jnp.where(first_valid, down_pair[0], empty)
        upper_second = jnp.where(second_valid, down_pair[1], empty)
        a_term = product(a_first, upper_first) + product(a_second, upper_second)
        b_term = product(across_pair[0], b_first) + product(across_pair[1], b_second)
        return rhs - (a_term + b_term)

    tail = lax.cond(on_trail, update_trail, lambda: rhs)
    return jnp.where(on_first, first_x, jnp.where(on_second, second_x, tail))


def solution(mesh):
    placed = (P("row", "col"), P("row", "col"), P("row", "col"), P("row", None), P(None, "col"))
    return jax.shard_map(
        body, mesh=mesh, in_specs=placed, out_specs=P("row", "col"), check_vma=False
    )
```

profile of v0, /device:TPU:102, one launch (start us, length us, event | category | flops | bytes accessed | tf_op | source)
XLA Modules:
  0.0 715.6 jit_solution(4404233032780703714)
XLA Ops:
  6.5 1.2 copy.43
  7.7 0.1 copy-done.1
  7.8 0.2 copy-done
  8.0 9.1 %conditional.3 = (f32[384,384]{1,0:T(8,128)S(1)}) conditional(s32[]{:T(128)} %convert_element_type.14, () %tuple.25, (f32[384,384]{1,0:T(8,128)S(1)}, f32[384,384]{1,0:T(8,128)S(1)}, f32[384,384]{1,0:T(8,128)S(1)}) %tuple.59), branch_computations={%region_0.0_spmd, %region_1.0_spmd} | conditional | flops 8154611712 | bytes 20643848 | solution.py:49
  17.0 1.2 broadcast_select_fusion.3
  18.3 0.7 all-reduce.5.cloned.1.call-update
  19.1 1.1 slice.16
  20.2 1.1 slice.17
  21.3 207.7 %all-reduce.7.cloned.1.call-done = f32[384,384]{1,0:T(8,128)} async-done(((f32[384,384]{1,0:T(8,128)}), f32[384,384]{1,0:T(8,128)}) %all-reduce.7.cloned.1.call-update) | async-done | bytes 589840 | tf_op jit(solution)/shard_map/psum | solution.py:12
  229.0 121.1 %all-reduce.5.cloned.1.call-done = f32[384,384]{1,0:T(8,128)} async-done(((f32[384,384]{1,0:T(8,128)}), f32[384,384]{1,0:T(8,128)}) %all-reduce.5.cloned.1.call-update) | async-done | bytes 589840 | tf_op jit(solution)/shard_map/psum | solution.py:12
  350.1 5.9 conditional.4
  356.0 1.1 broadcast_select_fusion
  357.2 0.5 all-reduce.9.cloned.1.call-update
  357.7 215.8 %all-reduce.11.cloned.1.call-done = f32[384,384]{1,0:T(8,128)} async-done(((f32[384,384]{1,0:T(8,128)}), f32[384,384]{1,0:T(8,128)}) %all-reduce.11.cloned.1.call-update) | async-done | bytes 589840 | tf_op jit(solution)/shard_map/psum | solution.py:12
  573.5 120.9 %all-reduce.9.cloned.1.call-done = f32[384,384]{1,0:T(8,128)} async-done(((f32[384,384]{1,0:T(8,128)}), f32[384,384]{1,0:T(8,128)}) %all-reduce.9.cloned.1.call-update) | async-done | bytes 589840 | tf_op jit(solution)/shard_map/psum | solution.py:12
  694.4 13.3 %conditional.5 = ((f32[384,384]{1,0:T(8,128)S(1)})) conditional(s32[]{:T(128)} %convert_element_type.16, (f32[384,384]{1,0:T(8,128)S(1)}) %tuple.38, (s32[]{:T(128)}, f32[384,384]{1,0:T(8,128)}, f32[384,384]{1,0:T(8,128)S(1)}, s32[]{:T(128)}, f32[384,384]{1,0:T(8,128)}, /*index=5*/f32[384,768]{1,0:T(8,128)}, f32[384,384]{1,0:T(8,128)S(1)}, ...), branch_computations={%region_8.9_spmd, %region_9.10_spmd} | conditional | flops 2718793728 | bytes 18874484 | solution.py:81
  694.4 4.0 fusion.8
  698.4 1.3 fusion.29
  699.7 3.2 convolution_add_fusion.4
  703.0 0.2 copy.17
  703.2 0.8 copy-done.6
  704.0 3.5 fusion.4
  707.5 0.2 copy.30
  707.7 0.9 select_select_fusion
  (20 shorter events, 0.3 us)
Async XLA Ops:
  6.5 1.2 copy-start.1
  6.5 1.4 copy-start
  6.5 222.4 %all-reduce.7.cloned.1.call-start = ((), (), s32[]{:S(2)}) async-start(), calls=%async_computation.1 | async-start | bytes 1179648 | tf_op jit(solution)/shard_map/psum | solution.py:12
  17.0 1.2 copy-start.2
  18.2 331.8 %all-reduce.5.cloned.1.call-start = ((), (), s32[]{:S(2)}) async-start(), calls=%async_computation | async-start | bytes 1179648 | tf_op jit(solution)/shard_map/psum | solution.py:12
  19.0 554.5 %all-reduce.11.cloned.1.call-start = ((), (), s32[]{:S(2)}) async-start(), calls=%async_computation.3 | async-start | bytes 1179648 | tf_op jit(solution)/shard_map/psum | solution.py:12
  356.0 338.4 %copy-start.4 = (f32[384,384]{1,0:T(8,128)S(1)}, f32[384,384]{1,0:T(8,128)}, u32[]{:S(2)}) copy-start(f32[384,384]{1,0:T(8,128)} %all-reduce.7.cloned.1.call-done) | copy-start | bytes 1769476
  357.1 337.3 %all-reduce.9.cloned.1.call-start = ((), (), s32[]{:S(2)}) async-start(), calls=%async_computation.2 | async-start | bytes 1179648 | tf_op jit(solution)/shard_map/psum | solution.py:12
  694.4 13.3 %copy-start.3 = (f32[384,384]{1,0:T(8,128)S(1)}, f32[384,384]{1,0:T(8,128)}, u32[]{:S(2)}) copy-start(f32[384,384]{1,0:T(8,128)} %copy-done.2) | copy-start | bytes 1769476
  698.4 1.3 copy-start.7
  703.0 1.1 copy-start.6
Sparse Core Ops, SparseCore 0:
  18.4 210.5 all-reduce.6
  232.2 117.7 all-reduce.4
  357.2 216.2 all-reduce.10
  576.6 117.7 all-reduce.8
where the time goes:
time: 725 us; the launch traced here: 716 us
  waiting for transfers between devices  667 us (92%)
  loops' own time  14.9 us (2%)
  between operations  13.7 us (2%)
  matrix products  12 us (2%)
    psum x4, waiting for transfers between devices, from_root(): return lax.psum(kept, axis)  665 us
  transfers between devices with their start and end apart: 4, of which 4 were waited for; matrix products, arithmetic and copies ran while one was open for 0% of the time, Pallas kernels for 0%

commit v1 on v0

--- a/solution.py
+++ b/solution.py
@@ -7,9 +7,15 @@
 precise = lax.Precision.HIGHEST
 
 
+def summed_here(array, mesh_axis):
+    terms = lax.all_gather(array, mesh_axis, axis=0, tiled=False)
+    total = terms.sum(axis=0)
+    return total
+
+
 def from_root(value, axis, source):
     kept = jnp.where(lax.axis_index(axis) == source, value, 0).astype(value.dtype)
-    return lax.psum(kept, axis)
+    return summed_here(kept, axis)
 
 
 def product(left_side, right_side):

time: 725 us -> 564 us (0.78)
  waiting for transfers between devices: 667 us -> 441 us
  local copies, waits for them, and re-layouts: 5.05 us -> 49.9 us
  other arithmetic: 3.2 us -> 27 us
    psum x4 -> x0, waiting for transfers between devices: 665 us -> none  [from_root(): return lax.psum(kept, axis)]
    all_gather x0 -> x4, waiting for transfers between devices: none -> 440 us  [summed_here(): terms = lax.all_gather(array, mesh_axis, axis=0, tiled=False)]
    reduce_sum x0 -> x4, other arithmetic: none -> 23.9 us  [summed_here(): total = terms.sum(axis=0)]
    cond x4 -> x6, local copies, waits for them, and re-layouts: 0.84 us -> 22.8 us
    unnamed x11 -> x15, local copies, waits for them, and re-layouts: 1.43 us -> 22.4 us
  transfers between devices with their start and end apart: 4 -> 4, of which waited for: 4 -> 4; matrix products, arithmetic and copies ran while one was open for 0% -> 2% of each run, Pallas kernels for 0% -> 0%
where the time goes in v1:
time: 564 us; the launch traced here: 554 us
  waiting for transfers between devices  441 us (78%)
  local copies, waits for them, and re-layouts  49.9 us (9%)
  other arithmetic  27 us (5%)
  between operations  13.8 us (2%)
  matrix products  12 us (2%)
  loops' own time  10.5 us (2%)
    all_gather x4, waiting for transfers between devices, summed_here(): terms = lax.all_gather(array, mesh_axis, axis=0, tiled=False)  440 us
    reduce_sum x4, other arithmetic, summed_here(): total = terms.sum(axis=0)  23.9 us
    unnamed x15, local copies, waits for them, and re-layouts  22.4 us
    cond x4, local copies, waits for them, and re-layouts  21.5 us
    dot_general x4, matrix products, product(): jnp.dot(left_side, right_side, precision=precise, preferred_element_type=...  12 us
  transfers between devices with their start and end apart: 4, of which 4 were waited for; matrix products, arithmetic and copies ran while one was open for 2% of the time, Pallas kernels for 0%

profile of v1, /device:TPU:102, one launch (start us, length us, event | category | flops | bytes accessed | tf_op | source)
XLA Modules:
  0.0 554.1 jit_solution(16328555725577389227)
XLA Ops:
  6.5 1.1 copy.70
  7.6 7.5 %conditional.3 = (f32[384,384]{1,0:T(8,128)S(1)}) conditional(s32[]{:T(128)} %convert_element_type.14, () %tuple.23, (f32[384,384]{1,0:T(8,128)}, f32[384,384]{1,0:T(8,128)S(1)}, f32[384,384]{1,0:T(8,128)}) %tuple.24), branch_computations={%region_0.0_spmd, %region_1.0_spmd} | conditional | flops 8154611712 | bytes 23003172 | solution.py:55
  15.4 1.1 broadcast_select_fusion.3
  17.3 1.9 slice.12
  20.2 102.2 %all-gather.11.cloned.1.call-done = f32[6144,384]{0,1:T(8,128)} async-done(((f32[384,384]{0,1:T(8,128)}), f32[6144,384]{0,1:T(8,128)}) %all-gather.11.cloned.1.call-update) | async-done | bytes 9437200 | tf_op jit(solution)/shard_map/all_gather | solution.py:11
  122.4 5.7 %copy.62 = f32[48,8,16,384]{3,2,1,0:T(8,128)S(1)} copy(f32[48,8,16,384]{3,1,2,0:T(8,128)} %bitcast.99) | data formatting | bytes 18874368
  128.1 2.2 bitcast_reduce_fusion.3
  130.2 110.0 %all-gather.9.cloned.1.call-done = f32[12288,384]{0,1:T(8,128)} async-done(((f32[384,384]{0,1:T(8,128)}), f32[12288,384]{0,1:T(8,128)}) %all-gather.9.cloned.1.call-update) | async-done | bytes 18874384 | tf_op jit(solution)/shard_map/all_gather | solution.py:11
  240.2 15.6 %copy.61 = f32[48,8,32,384]{3,2,1,0:T(8,128)} copy(f32[48,8,32,384]{3,1,2,0:T(8,128)} %bitcast.97) | data formatting | bytes 37748736
  255.9 9.7 %bitcast_reduce_fusion.2 = f32[384,384]{0,1:T(8,128)S(1)} fusion(f32[48,8,32,384]{3,2,1,0:T(8,128)} %copy.61), kind=kLoop, calls=%fused_computation.38 | loop fusion | flops 4571136 | bytes 19464192 | tf_op jit(solution)/shard_map/reduce_sum | solution.py:12
  266.4 2.7 conditional.4
  269.1 1.1 broadcast_select_fusion
  270.8 1.1 copy.40
  271.9 109.6 %all-gather.13.cloned.1.call-done = f32[6144,384]{0,1:T(8,128)} async-done(((f32[384,384]{0,1:T(8,128)}), f32[6144,384]{0,1:T(8,128)}) %all-gather.13.cloned.1.call-update) | async-done | bytes 9437200 | tf_op jit(solution)/shard_map/all_gather | solution.py:11
  381.5 117.7 %all-gather.15.cloned.1.call-done = f32[12288,384]{0,1:T(8,128)} async-done(((f32[384,384]{0,1:T(8,128)}), f32[12288,384]{0,1:T(8,128)}) %all-gather.15.cloned.1.call-update) | async-done | bytes 18874384 | tf_op jit(solution)/shard_map/all_gather | solution.py:11
  499.2 46.9 %conditional.5 = ((f32[384,384]{1,0:T(8,128)S(1)})) conditional(s32[]{:T(128)} %convert_element_type.16, (f32[384,384]{1,0:T(8,128)S(1)}) %tuple.36, (s32[]{:T(128)}, f32[384,384]{0,1:T(8,128)S(1)}, f32[384,384]{1,0:T(8,128)}, s32[]{:T(128)}, f32[6144,384]{0,1:T(8,128)}, /*index=5*/f32[384,768]{1,0:T(8,128)}, f32[384,384]{0,1:T(8,128)S(1)}, ...), branch_computations={%region_8.9_spmd, %region_9.10_spmd.clone} | conditional | flops 2725576704 | bytes 102629472 | solution.py:87
  499.4 4.0 fusion.14
  503.5 15.9 %copy.60 = f32[48,8,32,384]{3,2,1,0:T(8,128)} copy(f32[48,8,32,384]{3,1,2,0:T(8,128)} %bitcast.96) | data formatting | bytes 37748736 | tf_op jit(solution)/shard_map/cond
  519.4 9.6 %bitcast_reduce_fusion = f32[384,384]{0,1:T(8,128)S(1)} fusion(f32[]{:T(128)} %get-tuple-element.169, f32[48,8,32,384]{3,2,1,0:T(8,128)} %copy.60), kind=kLoop, calls=%fused_computation.20 | loop fusion | flops 4571136 | bytes 19464196 | tf_op jit(solution)/shard_map/reduce_sum | solution.py:12
  529.0 1.3 fusion.36
  530.3 3.2 convolution_add_fusion.8
  533.5 5.6 %copy.59 = f32[48,8,16,384]{3,2,1,0:T(8,128)S(1)} copy(f32[48,8,16,384]{3,1,2,0:T(8,128)} %bitcast.98) | data formatting | bytes 18874368 | tf_op jit(solution)/shard_map/cond
  539.1 2.4 bitcast_reduce_fusion.1
  542.1 3.5 fusion.10
  (32 shorter events, 5.3 us)
Async XLA Ops:
  6.5 115.8 %all-gather.11.cloned.1.call-start = ((), (), s32[]{:S(2)}) async-start(), calls=%async_computation.1 | async-start | bytes 10027008 | tf_op jit(solution)/shard_map/all_gather | solution.py:11
  7.6 11.7 %copy-start.7 = (f32[768,384]{1,0:T(8,128)S(1)}, f32[768,384]{1,0:T(8,128)}, u32[]{:S(2)}) copy-start(f32[768,384]{1,0:T(8,128)} %param.13) | copy-start | bytes 3538948
  15.1 112.9 %copy-start.4 = (f32[384,384]{1,0:T(8,128)}, f32[384,384]{1,0:T(8,128)S(1)}, u32[]{:S(2)}) copy-start(f32[384,384]{1,0:T(8,128)S(1)} %get-tuple-element.205) | copy-start | bytes 1769476
  16.5 223.7 %all-gather.9.cloned.1.call-start = ((), (), s32[]{:S(2)}) async-start(), calls=%async_computation | async-start | bytes 19464192 | tf_op jit(solution)/shard_map/all_gather | solution.py:11
  17.3 364.2 %all-gather.13.cloned.1.call-start = ((), (), s32[]{:S(2)}) async-start(), calls=%async_computation.2 | async-start | bytes 10027008 | tf_op jit(solution)/shard_map/all_gather | solution.py:11
  255.9 10.5 %copy-start = (f32[384,384]{1,0:T(8,128)S(1)}, f32[384,384]{1,0:T(8,128)}, u32[]{:S(2)}) copy-start(f32[384,384]{1,0:T(8,128)} %param.15) | copy-start | bytes 1769476
  255.9 10.5 %copy-start.1 = (f32[384,384]{1,0:T(8,128)S(1)}, f32[384,384]{1,0:T(8,128)}, u32[]{:S(2)}) copy-start(f32[384,384]{1,0:T(8,128)} %param.14) | copy-start | bytes 1769476
  270.3 228.9 %all-gather.15.cloned.1.call-start = ((), (), s32[]{:S(2)}) async-start(), calls=%async_computation.3 | async-start | bytes 19464192 | tf_op jit(solution)/shard_map/all_gather | solution.py:11
  499.2 46.9 %copy-start.5 = (f32[384,384]{1,0:T(8,128)S(1)}, f32[384,384]{1,0:T(8,128)}, u32[]{:S(2)}) copy-start(f32[384,384]{1,0:T(8,128)} %copy-done.4) | copy-start | bytes 1769476
  499.2 46.9 %copy-start.6 = (f32[384,384]{1,0:T(8,128)S(1)}, f32[384,384]{1,0:T(8,128)}, u32[]{:S(2)}) copy-start(f32[384,384]{1,0:T(8,128)} %copy.40) | copy-start | bytes 1769476
  519.4 9.6 %copy-start.3 = (f32[384,384]{1,0:T(8,128)S(1)}, f32[384,384]{1,0:T(8,128)}, u32[]{:S(2)}) copy-start(f32[384,384]{1,0:T(8,128)} %get-tuple-element.167) | copy-start | bytes 1769476 | tf_op jit(solution)/shard_map/cond
Sparse Core Ops, SparseCore 0:
  16.7 105.6 all-gather.10
  124.5 115.6 all-gather.8
  270.4 111.0 all-gather.12
  383.5 115.6 all-gather.14
